TPU v7x, 256 devices: a whole 4x4x8 slice. The times are simulated.
256 devices in a mesh: grp: 16 (over z, core), ing: 16 (over y, x).
Axes of the slice: x: 4, y: 4, z: 8, core: 2. Of those that a mesh axis runs over, the one named last changes fastest.
Arguments:
- amplitudes: bfloat16 [512, 800, 800], P('grp', 'ing'), may hold values from -6 to 6
- integrals: bfloat16 [512, 800, 800], P('grp', 'ing'), may hold values from -0.0024414062 to 0.0024414062
- fock_block: bfloat16 [800, 800], P('ing'), may hold values from -0.625 to 0.625
- virtual_irrep: int32 [800], replicated, may hold values from 0 to 7, as said below
- pair_irrep: int32 [512], P(('grp', 'ing')), may hold values from 0 to 7
- pair_energy: float32 [512], P(('grp', 'ing')), may hold values from -4 to -1
- virtual_energy: float32 [800], replicated, may hold values from 0.5 to 4
Outputs:
- update: float32 [512, 800, 800], P('grp', 'ing')
Inputs may be any that keep to these rules, and one draw needn't show every extreme that they name: `virtual_irrep`: the orbitals of one irreducible representation form one contiguous run of 100 plus or minus at most 25 orbitals, and all 8 representations occur.
All inputs are finite; a program needn't handle non-finite values.
Results may differ from a plain program's by a relative error of at most 0.0029.
Values may be sent and summed in bfloat16 or wider, within the bound.
A program may use at most 128 MiB of HBM per device.

v0:
```python
import jax
import jax.numpy as jnp
from jax import lax
from jax.sharding import PartitionSpec as P


def symmetry_mask(values, pair_irrep, virtual_irrep):
    allowed = (
        jnp.bitwise_xor(virtual_irrep[:, None], virtual_irrep[None, :])[None]
        == pair_irrep[:, None, None]
    )
    return jnp.where(allowed, values, jnp.zeros_like(values))


def body(amplitudes, integrals, fock_block, virtual_irrep, pair_irrep, pair_energy, virtual_energy):
    same_irrep = virtual_irrep[:, None] == virtual_irrep[None, :]
    whole_amps, whole_ints = (
        lax.all_to_all(amplitudes, "ing", split_axis=0, concat_axis=1, tiled=True),
        lax.all_to_all(integrals, "ing", split_axis=0, concat_axis=1, tiled=True),
    )
    amp_masked = symmetry_mask(whole_amps, pair_irrep, virtual_irrep)
    int_masked = symmetry_mask(whole_ints, pair_irrep, virtual_irrep)
    partial_value = jnp.einsum(
        "paf,pef->ae", amp_masked, int_masked, preferred_element_type=jnp.float32
    )
    correction = lax.psum(partial_value, ("grp", "ing"))
    fock_full = lax.all_gather(fock_block, "ing", axis=0, tiled=True)
    fock_part = jnp.where(
        same_irrep, fock_full.astype(jnp.float32), jnp.zeros(fock_full.shape, jnp.float32)
    )
    operator_vv = (fock_part + correction).astype(jnp.bfloat16)
    product = jnp.einsum("pae,be->pab", amp_masked, operator_vv, preferred_element_type=jnp.float32)
    denominator = (
        pair_energy[:, None, None] - virtual_energy[None, :, None] - virtual_energy[None, None, :]
    )
    scaled = (product - jnp.swapaxes(product, 1, 2)) / denominator
    return lax.all_to_all(scaled, "ing", split_axis=1, concat_axis=0, tiled=True)


def solution(mesh):
    in_specs = (
        P("grp", "ing", None),
        P("grp", "ing", None),
        P("ing", None),
        P(),
        P(("grp", "ing")),
        P(("grp", "ing")),
        P(),
    )
    out_specs = P("grp", "ing", None)
    return jax.shard_map(body, mesh=mesh, in_specs=in_specs, out_specs=out_specs, check_vma=False)
```

profile of v0, /device:TPU:99, one launch (start us, length us, event | category | flops | bytes accessed | tf_op | source)
XLA Modules:
  0.0 516.4 jit_solution(2653213600742417975)
XLA Ops:
  7.4 4.4 copy.25
  11.8 6.9 %all-to-all-start = ((bf16[32,50,800]{2,1,0:T(8,128)(2,1)}), bf16[32,50,800]{2,1,0:T(8,128)(2,1)S(1)}, u32[]{:S(2)}, u32[]{:S(2)}) async-start(bf16[32,50,800]{2,1,0:T(8,128)(2,1)} %copy.25), calls=%async_computation | async-start | bytes 6422528 | tf_op jit(solution)/shard_map/all_to_all | solution.py:18
  18.7 4.5 copy.27
  23.2 39.1 %all-to-all-done = bf16[32,50,800]{2,1,0:T(8,128)(2,1)S(1)} async-done(((bf16[32,50,800]{2,1,0:T(8,128)(2,1)}), bf16[32,50,800]{2,1,0:T(8,128)(2,1)S(1)}, u32[]{:S(2)}, u32[]{:S(2)}) %all-to-all-start) | async-done | bytes 2560032 | tf_op jit(solution)/shard_map/all_to_all | solution.py:18
  62.3 8.3 %all-to-all-start.1 = ((bf16[32,50,800]{2,1,0:T(8,128)(2,1)}), bf16[32,50,800]{2,1,0:T(8,128)(2,1)}, u32[]{:S(2)}, u32[]{:S(2)}) async-start(bf16[32,50,800]{2,1,0:T(8,128)(2,1)} %copy.27), calls=%async_computation.1 | async-start | bytes 6422528 | tf_op jit(solution)/shard_map/all_to_all | solution.py:19
  70.7 0.7 all-gather.3.cloned.1.call-update
  71.5 1.8 broadcast_xor_fusion
  73.3 3.8 copy.26
  77.1 35.5 %all-to-all-done.1 = bf16[32,50,800]{2,1,0:T(8,128)(2,1)} async-done(((bf16[32,50,800]{2,1,0:T(8,128)(2,1)}), bf16[32,50,800]{2,1,0:T(8,128)(2,1)}, u32[]{:S(2)}, u32[]{:S(2)}) %all-to-all-start.1) | async-done | bytes 2560032 | tf_op jit(solution)/shard_map/all_to_all | solution.py:19
  112.6 4.3 copy.28
  116.9 7.2 %compare_select_fusion = (bf16[2,800,800]{2,0,1:T(2,128)(2,1)S(1)}, bf16[2,800,800]{2,0,1:T(2,128)(2,1)S(1)}) fusion(bf16[16,2,50,800]{3,1,2,0:T(2,128)(2,1)S(1)} %copy.28, s32[800,800]{1,0:T(8,128)S(1)} %copy-done, s32[2]{0:T(128)S(1)} %copy-done.4, bf16[16,2,50,800]{3,1,2,0:T(2,128)(2,1)S(1)} %copy-done.1), kind=kLoop, calls=%fused_computation | loop fusion | flops 3840000 | bytes 12800008 | tf_op jit(solution)/shard_map/jit(_where)/select_n | solution.py:12
  124.1 4.8 fusion.6
  129.0 0.7 copy-done.3
  129.7 0.1 broadcast_subtract_fusion
  129.7 9.6 %all-gather.3.cloned.1.call-done = bf16[16,50,800]{2,1,0:T(8,128)(2,1)} async-done(((bf16[1,50,800]{2,1,0:T(8,128)(2,1)}), bf16[16,50,800]{2,1,0:T(8,128)(2,1)}) %all-gather.3.cloned.1.call-update) | async-done | bytes 1280016 | tf_op jit(solution)/shard_map/all_gather | solution.py:27
  139.3 3.0 reshape.63
  142.4 254.5 %all-reduce.2.cloned.1.call-done = f32[800,800]{1,0:T(8,128)} async-done(((f32[800,800]{1,0:T(8,128)}), f32[800,800]{1,0:T(8,128)}) %all-reduce.2.cloned.1.call-update) | async-done | bytes 2560016 | tf_op jit(solution)/shard_map/psum | solution.py:26
  396.8 8.1 %fusion.4 = f32[2,800,800]{2,1,0:T(8,128)} fusion(bf16[2,800,800]{2,0,1:T(2,128)(2,1)S(1)} %get-tuple-element.6, f32[800,800]{1,0:T(8,128)} %all-reduce.2.cloned.1.call-done, f32[800,800]{1,0:T(8,128)} %reshape.63, s32[800]{0:T(1024)S(1)} %copy-done.2), kind=kOutput, calls=%fused_computation.8 | convolution fusion | flops 2050560000 | bytes 12803200 | tf_op jit(solution)/shard_map/pae,be->pab/dot_general | solution.py:32
  404.9 7.1 %copy.32 = f32[2,800,800]{1,2,0:T(8,128)} copy(f32[2,800,800]{2,1,0:T(8,128)} %fusion.4) | data formatting | bytes 10240000 | tf_op jit(solution)/shard_map/pae,be->pab/dot_general | solution.py:32
  412.0 5.1 fusion
  417.1 4.4 copy.33
  421.5 73.9 %all_to_all.54 = f32[2,800,800]{2,0,1:T(2,128)S(1)} all-to-all(f32[2,800,800]{2,0,1:T(2,128)S(1)} %copy.33), channel_id=1, replica_groups=mesh['grp'=16,'ing'=16] {'ing'}, dimensions={1} | all-to-all | bytes 10240000 | tf_op jit(solution)/shard_map/all_to_all | solution.py:37
  495.4 5.7 %copy.34 = f32[16,2,50,800]{3,1,0,2:T(2,128)} copy(f32[16,2,50,800]{3,1,2,0:T(2,128)S(1)} %bitcast.25) | data formatting | bytes 10240000 | tf_op jit(solution)/shard_map/all_to_all | solution.py:37
  501.1 7.8 %all_to_all.50 = f32[32,50,800]{2,0,1:T(8,128)} reshape(f32[16,2,50,800]{3,1,0,2:T(2,128)} %copy.34) | data formatting | bytes 10240000 | tf_op jit(solution)/shard_map/all_to_all | solution.py:37
  (14 shorter events, 0.1 us)
Async XLA Ops:
  11.8 50.5 %all-to-all-start = ((bf16[32,50,800]{2,1,0:T(8,128)(2,1)}), bf16[32,50,800]{2,1,0:T(8,128)(2,1)S(1)}, u32[]{:S(2)}, u32[]{:S(2)}) async-start(bf16[32,50,800]{2,1,0:T(8,128)(2,1)} %copy.25), calls=%async_computation | async-start | bytes 6422528 | tf_op jit(solution)/shard_map/all_to_all | solution.py:18
  23.2 48.2 %copy-start.2 = (s32[800]{0:T(1024)S(1)}, s32[800]{0:T(1024)}, u32[]{:S(2)}) copy-start(s32[800]{0:T(1024)} %param.10) | copy-start | bytes 9604
  62.3 50.3 %all-to-all-start.1 = ((bf16[32,50,800]{2,1,0:T(8,128)(2,1)}), bf16[32,50,800]{2,1,0:T(8,128)(2,1)}, u32[]{:S(2)}, u32[]{:S(2)}) async-start(bf16[32,50,800]{2,1,0:T(8,128)(2,1)} %copy.27), calls=%async_computation.1 | async-start | bytes 6422528 | tf_op jit(solution)/shard_map/all_to_all | solution.py:19
  70.7 68.7 %all-gather.3.cloned.1.call-start = ((), (), s32[]{:S(2)}) async-start(), calls=%async_computation.4 | async-start | bytes 1705984 | tf_op jit(solution)/shard_map/all_gather | solution.py:27
  71.4 325.4 %all-reduce.2.cloned.1.call-start = ((), (), s32[]{:S(2)}) async-start(), calls=%async_computation.3 | async-start | bytes 5734400 | tf_op jit(solution)/shard_map/psum | solution.py:26
  112.6 4.3 copy-start
  112.6 4.3 copy-start.1
  112.6 4.3 copy-start.4
  129.0 0.7 copy-start.3
  129.0 0.7 copy-start.5
Sparse Core Ops, SparseCore 0:
  74.2 65.0 all-gather.2
Sparse Core Ops, SparseCore 1:
  129.1 267.7 all-reduce.1
where the time goes:
time: 517 us; the launch traced here: 516 us
  waiting for transfers between devices  339 us (66%)
  blocking collectives  73.9 us (14%)
  local copies, waits for them, and re-layouts  45.7 us (9%)
  starting transfers between devices  15.3 us (3%)
  between operations  14.9 us (3%)
  other arithmetic  14.3 us (3%)
  matrix products  12.9 us (2%)
    psum x1, waiting for transfers between devices, body(): correction = lax.psum(partial_value, ('grp', 'ing'))  254 us
    all_to_all x1, blocking collectives, body(): lax.all_to_all(scaled, 'ing', split_axis=1, concat_axis=0, tiled=True)  73.9 us
    all_to_all x1, waiting for transfers between devices, body(): lax.all_to_all(amplitudes, 'ing', split_axis=0, concat_axis=1, tiled=True)  39.1 us
    all_to_all x1, waiting for transfers between devices, body(): lax.all_to_all(integrals, 'ing', split_axis=0, concat_axis=1, tiled=True)  35.5 us
    all_to_all x2, local copies, waits for them, and re-layouts, body(): lax.all_to_all(scaled, 'ing', split_axis=1, concat_axis=0, tiled=True)  13.5 us
  transfers between devices with their start and end apart: 4, of which 4 were waited for; matrix products, arithmetic and copies ran while one was open for 6% of the time, Pallas kernels for 0%

commit v1 on v0

--- a/solution.py
+++ b/solution.py
@@ -2,6 +2,28 @@
 import jax.numpy as jnp
 from jax import lax
 from jax.sharding import PartitionSpec as P
+
+
+def split_up(array, dim, length):
+    before, after = (array.shape[:dim], array.shape[dim + 1 :])
+    return jnp.moveaxis(array.reshape(*before, length, -1, *after), dim, 0)
+
+
+def laid_out(pieces, dim):
+    dims = list(pieces.shape[1:])
+    dims[dim] *= pieces.shape[0]
+    return jnp.moveaxis(pieces, 0, dim).reshape(dims)
+
+
+def exchange_in_pairs(x, axis, split_dim, concat_dim):
+    size, index = (lax.axis_size(axis), lax.axis_index(axis))
+    blocks = split_up(x, split_dim, size)
+    outs = [blocks[index]]
+    for hop in range(1, size):
+        sent = blocks[index ^ hop]
+        outs.append(lax.ppermute(sent, axis, [(i, i ^ hop) for i in range(size)]))
+    blocks = jnp.stack(outs)[index ^ jnp.arange(size)]
+    return laid_out(blocks, concat_dim)
 
 
 def symmetry_mask(values, pair_irrep, virtual_irrep):
@@ -16,7 +38,7 @@
     same_irrep = virtual_irrep[:, None] == virtual_irrep[None, :]
     whole_amps, whole_ints = (
         lax.all_to_all(amplitudes, "ing", split_axis=0, concat_axis=1, tiled=True),
-        lax.all_to_all(integrals, "ing", split_axis=0, concat_axis=1, tiled=True),
+        exchange_in_pairs(integrals, "ing", 0, 1),
     )
     amp_masked = symmetry_mask(whole_amps, pair_irrep, virtual_irrep)
     int_masked = symmetry_mask(whole_ints, pair_irrep, virtual_irrep)

time: 517 us -> 541 us (1.046); the launches traced: 516 us -> 532 us
  waiting for transfers between devices: 339 us -> 302 us
  starting transfers between devices: 15.3 us -> 46.4 us
  local copies, waits for them, and re-layouts: 45.7 us -> 67.3 us
    all_to_all x1, waiting for transfers between devices: 39.1 us -> 0.01 us  [body(): lax.all_to_all(amplitudes, 'ing', split_axis=0, concat_axis=1, tiled=True)]
    ppermute x0 -> x15, starting transfers between devices: none -> 38.6 us  [exchange_in_pairs(): outs.append(lax.ppermute(sent, axis, [(i, i ^ hop) for i in range(size)]))]
    all_to_all x1 -> x0, waiting for transfers between devices: 35.5 us -> none  [body(): lax.all_to_all(integrals, 'ing', split_axis=0, concat_axis=1, tiled=True)]
    ppermute x0 -> x15, waiting for transfers between devices: none -> 28.2 us  [exchange_in_pairs(): outs.append(lax.ppermute(sent, axis, [(i, i ^ hop) for i in range(size)]))]
    psum x1, waiting for transfers between devices: 254 us -> 273 us  [body(): correction = lax.psum(partial_value, ('grp', 'ing'))]
    all_gather x1, waiting for transfers between devices: 9.61 us -> 0.01 us  [body(): fock_full = lax.all_gather(fock_block, 'ing', axis=0, tiled=True)]
    gather x0 -> x1, local copies, waits for them, and re-layouts: none -> 8.84 us  [exchange_in_pairs(): blocks = jnp.stack(outs)[index ^ jnp.arange(size)]]
    all_to_all x1 -> x0, starting transfers between devices: 8.32 us -> none  [body(): lax.all_to_all(integrals, 'ing', split_axis=0, concat_axis=1, tiled=True)]
  transfers between devices with their start and end apart: 4 -> 18, of which waited for: 4 -> 4; matrix products, arithmetic and copies ran while one was open for 6% -> 8% of each run, Pallas kernels for 0% -> 0%
where the time goes in v1:
time: 541 us; the launch traced here: 532 us
  waiting for transfers between devices  302 us (56%)
  blocking collectives  73.9 us (14%)
  local copies, waits for them, and re-layouts  67.3 us (12%)
  starting transfers between devices  46.4 us (9%)
  between operations  15.5 us (3%)
  other arithmetic  14.1 us (3%)
  matrix products  12.8 us (2%)
    psum x1, waiting for transfers between devices, body(): correction = lax.psum(partial_value, ('grp', 'ing'))  273 us
    all_to_all x1, blocking collectives, body(): lax.all_to_all(scaled, 'ing', split_axis=1, concat_axis=0, tiled=True)  73.9 us
    ppermute x15, starting transfers between devices, exchange_in_pairs(): outs.append(lax.ppermute(sent, axis, [(i, i ^ hop) for i in range(size)]))  38.6 us
    ppermute x15, waiting for transfers between devices, exchange_in_pairs(): outs.append(lax.ppermute(sent, axis, [(i, i ^ hop) for i in range(size)]))  28.2 us
    unnamed x45, local copies, waits for them, and re-layouts  16.4 us
    all_to_all x2, local copies, waits for them, and re-layouts, body(): lax.all_to_all(scaled, 'ing', split_axis=1, concat_axis=0, tiled=True)  13.5 us
  transfers between devices with their start and end apart: 18, of which 4 were waited for; matrix products, arithmetic and copies ran while one was open for 8% of the time, Pallas kernels for 0%

profile of v1, /device:TPU:99, one launch (start us, length us, event | category | flops | bytes accessed | tf_op | source)
XLA Modules:
  0.0 531.9 jit_solution(3471019632725271473)
XLA Ops:
  7.4 5.7 %reshape.83 = bf16[16,2,50,800]{3,1,0,2:T(2,128)(2,1)S(1)} reshape(bf16[32,50,800]{2,0,1:T(8,128)(2,1)} %param.8) | data formatting | bytes 5120000 | tf_op jit(solution)/shard_map/reshape | solution.py:9
  13.1 3.1 dynamic-slice_bitcast_fusion
  21.5 2.7 copy.23
  24.2 7.7 %all-to-all-start = ((bf16[32,50,800]{2,1,0:T(8,128)(2,1)}), bf16[32,50,800]{2,1,0:T(8,128)(2,1)}, u32[]{:S(2)}, u32[]{:S(2)}) async-start(bf16[32,50,800]{2,1,0:T(8,128)(2,1)} %copy.23), calls=%async_computation | async-start | bytes 6422528 | tf_op jit(solution)/shard_map/all_to_all | solution.py:40
  34.6 2.8 collective-permute-start.5
  39.0 2.4 collective-permute-start.7
  45.4 3.0 collective-permute-start.9
  49.2 24.7 %collective-permute-done.5 = bf16[2,50,800]{2,0,1:T(2,128)(2,1)S(1)} collective-permute-done((bf16[2,50,800]{2,0,1:T(2,128)(2,1)S(1)}, bf16[2,50,800]{2,0,1:T(2,128)(2,1)S(1)}, u32[]{:S(2)}, u32[]{:S(2)}) %collective-permute-start.5) | collective-permute-done | bytes 160032 | tf_op jit(solution)/shard_map/ppermute | solution.py:24
  74.0 14.3 %collective-permute-start.10 = (bf16[2,50,800]{2,0,1:T(2,128)(2,1)S(1)}, bf16[2,50,800]{2,0,1:T(2,128)(2,1)S(1)}, u32[]{:S(2)}, u32[]{:S(2)}) collective-permute-start(bf16[2,50,800]{2,0,1:T(2,128)(2,1)S(1)} %copy-done.5), channel_id=1, source_target_pairs={{0,11},{1,10},{2,9},{3,8},{4,15},{5,14},{6,13},{7,12},{8,3},{9,2},... | collective-permute-start | bytes 480008 | tf_op jit(solution)/shard_map/ppermute | solution.py:24
  90.1 5.0 collective-permute-start.12
  105.1 2.5 collective-permute-done.14
  108.4 8.8 %gather_fusion = bf16[16,2,50,800]{3,1,2,0:T(2,128)(2,1)S(1)} fusion(bf16[16,2,50,800]{3,1,0,2:T(2,128)(2,1)} %bitcast_dynamic-update-slice_fusion, s32[1024]{0:T(1024)S(1)} %pad_clamp_fusion), kind=kCustom, calls=%fused_computation | custom fusion | bytes 5120064 | tf_op jit(solution)/shard_map/gather | solution.py:25
  117.3 4.3 copy.24
  121.6 7.1 %compare_select_fusion = (bf16[2,800,800]{2,0,1:T(2,128)(2,1)S(1)}, bf16[2,800,800]{2,0,1:T(2,128)(2,1)S(1)}) fusion(bf16[16,2,50,800]{3,1,2,0:T(2,128)(2,1)S(1)} %gather_fusion, s32[800,800]{1,0:T(8,128)S(1)} %copy-done, s32[2]{0:T(128)S(1)} %copy-done.13, bf16[16,2,50,800]{3,1,2,0:T(2,128)(2,1)S(1)} %copy.24), kind=kLoop, calls=%fused_computation.1 | loop fusion | flops 3840000 | bytes 12800008 | tf_op jit(solution)/shard_map/jit(_where)/select_n | solution.py:34
  130.3 4.7 fusion.6
  135.8 3.2 reshape.95
  139.0 273.0 %all-reduce.2.cloned.1.call-done = f32[800,800]{1,0:T(8,128)} async-done(((f32[800,800]{1,0:T(8,128)}), f32[800,800]{1,0:T(8,128)}) %all-reduce.2.cloned.1.call-update) | async-done | bytes 2560016 | tf_op jit(solution)/shard_map/psum | solution.py:48
  411.9 8.1 %fusion.4 = f32[2,800,800]{2,1,0:T(8,128)} fusion(bf16[2,800,800]{2,0,1:T(2,128)(2,1)S(1)} %copy-done.2, f32[800,800]{1,0:T(8,128)} %all-reduce.2.cloned.1.call-done, f32[800,800]{1,0:T(8,128)} %reshape.95, s32[800]{0:T(1024)S(1)} %copy-done.11), kind=kOutput, calls=%fused_computation.9 | convolution fusion | flops 2050560000 | bytes 12803200 | tf_op jit(solution)/shard_map/pae,be->pab/dot_general | solution.py:54
  420.0 7.1 %copy.28 = f32[2,800,800]{1,2,0:T(8,128)} copy(f32[2,800,800]{2,1,0:T(8,128)} %fusion.4) | data formatting | bytes 10240000 | tf_op jit(solution)/shard_map/pae,be->pab/dot_general | solution.py:54
  427.1 5.1 fusion
  432.2 4.4 copy.29
  436.6 73.9 %all_to_all.36 = f32[2,800,800]{2,0,1:T(2,128)S(1)} all-to-all(f32[2,800,800]{2,0,1:T(2,128)S(1)} %copy.29), channel_id=1, replica_groups=mesh['grp'=16,'ing'=16] {'ing'}, dimensions={1} | all-to-all | bytes 10240000 | tf_op jit(solution)/shard_map/all_to_all | solution.py:59
  510.5 5.7 %copy.30 = f32[16,2,50,800]{3,1,0,2:T(2,128)} copy(f32[16,2,50,800]{3,1,2,0:T(2,128)S(1)} %bitcast.88) | data formatting | bytes 10240000 | tf_op jit(solution)/shard_map/all_to_all | solution.py:59
  516.2 7.8 %all_to_all.33 = f32[32,50,800]{2,0,1:T(8,128)} reshape(f32[16,2,50,800]{3,1,0,2:T(2,128)} %copy.30) | data formatting | bytes 10240000 | tf_op jit(solution)/shard_map/all_to_all | solution.py:59
  (78 shorter events, 29.3 us)
Async XLA Ops:
  16.2 18.4 %collective-permute-start = (bf16[2,50,800]{2,0,1:T(2,128)(2,1)}, bf16[2,50,800]{2,0,1:T(2,128)(2,1)S(1)}, u32[]{:S(2)}, u32[]{:S(2)}) collective-permute-start(bf16[2,50,800]{2,0,1:T(2,128)(2,1)} %get-tuple-element.21), channel_id=1, source_target_pairs={{0,1},{1,0},{2,3},{3,2},{4,5},{5,4},{6,7},{7,6},{8,9},{9,8},{10,11... | collective-permute-start | bytes 480008 | tf_op jit(solution)/shard_map/ppermute | solution.py:24
  16.5 21.7 %collective-permute-start.1 = (bf16[2,50,800]{2,0,1:T(2,128)(2,1)}, bf16[2,50,800]{2,0,1:T(2,128)(2,1)S(1)}, u32[]{:S(2)}, u32[]{:S(2)}) collective-permute-start(bf16[2,50,800]{2,0,1:T(2,128)(2,1)} %get-tuple-element.20), channel_id=1, source_target_pairs={{0,2},{1,3},{2,0},{3,1},{4,6},{5,7},{6,4},{7,5},{8,10},{9,11},{10,... | collective-permute-start | bytes 480008 | tf_op jit(solution)/shard_map/ppermute | solution.py:24
  18.6 20.4 %collective-permute-start.2 = (bf16[2,50,800]{2,0,1:T(2,128)(2,1)}, bf16[2,50,800]{2,0,1:T(2,128)(2,1)S(1)}, u32[]{:S(2)}, u32[]{:S(2)}) collective-permute-start(bf16[2,50,800]{2,0,1:T(2,128)(2,1)} %get-tuple-element.19), channel_id=1, source_target_pairs={{0,3},{1,2},{2,1},{3,0},{4,7},{5,6},{6,5},{7,4},{8,11},{9,10},{10,... | collective-permute-start | bytes 480008 | tf_op jit(solution)/shard_map/ppermute | solution.py:24
  18.9 23.4 %collective-permute-start.3 = (bf16[2,50,800]{2,0,1:T(2,128)(2,1)}, bf16[2,50,800]{2,0,1:T(2,128)(2,1)S(1)}, u32[]{:S(2)}, u32[]{:S(2)}) collective-permute-start(bf16[2,50,800]{2,0,1:T(2,128)(2,1)} %get-tuple-element.18), channel_id=1, source_target_pairs={{0,4},{1,5},{2,6},{3,7},{4,0},{5,1},{6,2},{7,3},{8,12},{9,13},{10,... | collective-permute-start | bytes 480008 | tf_op jit(solution)/shard_map/ppermute | solution.py:24
  20.2 25.3 %collective-permute-start.4 = (bf16[2,50,800]{2,0,1:T(2,128)(2,1)}, bf16[2,50,800]{2,0,1:T(2,128)(2,1)S(1)}, u32[]{:S(2)}, u32[]{:S(2)}) collective-permute-start(bf16[2,50,800]{2,0,1:T(2,128)(2,1)} %get-tuple-element.17), channel_id=1, source_target_pairs={{0,5},{1,4},{2,7},{3,6},{4,1},{5,0},{6,3},{7,2},{8,13},{9,12},{10,... | collective-permute-start | bytes 480008 | tf_op jit(solution)/shard_map/ppermute | solution.py:24
  24.2 8.6 %copy-start.11 = (s32[800]{0:T(1024)S(1)}, s32[800]{0:T(1024)}, u32[]{:S(2)}) copy-start(s32[800]{0:T(1024)} %param.10) | copy-start | bytes 9604
  24.2 93.1 %all-to-all-start = ((bf16[32,50,800]{2,1,0:T(8,128)(2,1)}), bf16[32,50,800]{2,1,0:T(8,128)(2,1)}, u32[]{:S(2)}, u32[]{:S(2)}) async-start(bf16[32,50,800]{2,1,0:T(8,128)(2,1)} %copy.23), calls=%async_computation | async-start | bytes 6422528 | tf_op jit(solution)/shard_map/all_to_all | solution.py:40
  31.9 10.4 %copy-start.7 = (bf16[2,50,800]{2,0,1:T(2,128)(2,1)S(1)}, bf16[2,50,800]{2,0,1:T(2,128)(2,1)}, u32[]{:S(2)}) copy-start(bf16[2,50,800]{2,0,1:T(2,128)(2,1)} %get-tuple-element.13) | copy-start | bytes 480004
  31.9 13.5 %copy-start.6 = (bf16[2,50,800]{2,0,1:T(2,128)(2,1)S(1)}, bf16[2,50,800]{2,0,1:T(2,128)(2,1)}, u32[]{:S(2)}) copy-start(bf16[2,50,800]{2,0,1:T(2,128)(2,1)} %get-tuple-element.12) | copy-start | bytes 480004
  31.9 42.0 %copy-start.5 = (bf16[2,50,800]{2,0,1:T(2,128)(2,1)S(1)}, bf16[2,50,800]{2,0,1:T(2,128)(2,1)}, u32[]{:S(2)}) copy-start(bf16[2,50,800]{2,0,1:T(2,128)(2,1)} %get-tuple-element.11) | copy-start | bytes 480004
  31.9 57.2 %copy-start.4 = (bf16[2,50,800]{2,0,1:T(2,128)(2,1)S(1)}, bf16[2,50,800]{2,0,1:T(2,128)(2,1)}, u32[]{:S(2)}) copy-start(bf16[2,50,800]{2,0,1:T(2,128)(2,1)} %get-tuple-element.10) | copy-start | bytes 480004
  32.0 103.8 %all-gather.3.cloned.1.call-start = ((), (), s32[]{:S(2)}) async-start(), calls=%async_computation.3 | async-start | bytes 1705984 | tf_op jit(solution)/shard_map/all_gather | solution.py:49
  32.7 379.2 %all-reduce.2.cloned.1.call-start = ((), (), s32[]{:S(2)}) async-start(), calls=%async_computation.2 | async-start | bytes 5734400 | tf_op jit(solution)/shard_map/psum | solution.py:48
  34.6 39.4 %collective-permute-start.5 = (bf16[2,50,800]{2,0,1:T(2,128)(2,1)S(1)}, bf16[2,50,800]{2,0,1:T(2,128)(2,1)S(1)}, u32[]{:S(2)}, u32[]{:S(2)}) collective-permute-start(bf16[2,50,800]{2,0,1:T(2,128)(2,1)S(1)} %copy-done.10), channel_id=1, source_target_pairs={{0,6},{1,7},{2,4},{3,5},{4,2},{5,3},{6,0},{7,1},{8,14},{9,15},{10,... | collective-permute-start | bytes 480008 | tf_op jit(solution)/shard_map/ppermute | solution.py:24
  38.2 50.9 %collective-permute-start.6 = (bf16[2,50,800]{2,0,1:T(2,128)(2,1)S(1)}, bf16[2,50,800]{2,0,1:T(2,128)(2,1)S(1)}, u32[]{:S(2)}, u32[]{:S(2)}) collective-permute-start(bf16[2,50,800]{2,0,1:T(2,128)(2,1)S(1)} %copy-done.9), channel_id=1, source_target_pairs={{0,7},{1,6},{2,5},{3,4},{4,3},{5,2},{6,1},{7,0},{8,15},{9,14},{10,... | collective-permute-start | bytes 480008 | tf_op jit(solution)/shard_map/ppermute | solution.py:24
  39.0 51.1 %collective-permute-start.7 = (bf16[2,50,800]{2,0,1:T(2,128)(2,1)S(1)}, bf16[2,50,800]{2,0,1:T(2,128)(2,1)S(1)}, u32[]{:S(2)}, u32[]{:S(2)}) collective-permute-start(bf16[2,50,800]{2,0,1:T(2,128)(2,1)S(1)} %copy-done.8), channel_id=1, source_target_pairs={{0,8},{1,9},{2,10},{3,11},{4,12},{5,13},{6,14},{7,15},{8,0},{9,1},... | collective-permute-start | bytes 480008 | tf_op jit(solution)/shard_map/ppermute | solution.py:24
  42.3 53.6 %collective-permute-start.8 = (bf16[2,50,800]{2,0,1:T(2,128)(2,1)S(1)}, bf16[2,50,800]{2,0,1:T(2,128)(2,1)S(1)}, u32[]{:S(2)}, u32[]{:S(2)}) collective-permute-start(bf16[2,50,800]{2,0,1:T(2,128)(2,1)S(1)} %copy-done.7), channel_id=1, source_target_pairs={{0,9},{1,8},{2,11},{3,10},{4,13},{5,12},{6,15},{7,14},{8,1},{9,0},... | collective-permute-start | bytes 480008 | tf_op jit(solution)/shard_map/ppermute | solution.py:24
  45.4 53.6 %collective-permute-start.9 = (bf16[2,50,800]{2,0,1:T(2,128)(2,1)S(1)}, bf16[2,50,800]{2,0,1:T(2,128)(2,1)S(1)}, u32[]{:S(2)}, u32[]{:S(2)}) collective-permute-start(bf16[2,50,800]{2,0,1:T(2,128)(2,1)S(1)} %copy-done.6), channel_id=1, source_target_pairs={{0,10},{1,11},{2,8},{3,9},{4,14},{5,15},{6,12},{7,13},{8,2},{9,3},... | collective-permute-start | bytes 480008 | tf_op jit(solution)/shard_map/ppermute | solution.py:24
  74.0 26.9 %collective-permute-start.10 = (bf16[2,50,800]{2,0,1:T(2,128)(2,1)S(1)}, bf16[2,50,800]{2,0,1:T(2,128)(2,1)S(1)}, u32[]{:S(2)}, u32[]{:S(2)}) collective-permute-start(bf16[2,50,800]{2,0,1:T(2,128)(2,1)S(1)} %copy-done.5), channel_id=1, source_target_pairs={{0,11},{1,10},{2,9},{3,8},{4,15},{5,14},{6,13},{7,12},{8,3},{9,2},... | collective-permute-start | bytes 480008 | tf_op jit(solution)/shard_map/ppermute | solution.py:24
  89.2 12.6 %collective-permute-start.11 = (bf16[2,50,800]{2,0,1:T(2,128)(2,1)S(1)}, bf16[2,50,800]{2,0,1:T(2,128)(2,1)S(1)}, u32[]{:S(2)}, u32[]{:S(2)}) collective-permute-start(bf16[2,50,800]{2,0,1:T(2,128)(2,1)S(1)} %copy-done.4), channel_id=1, source_target_pairs={{0,12},{1,13},{2,14},{3,15},{4,8},{5,9},{6,10},{7,11},{8,4},{9,5},... | collective-permute-start | bytes 480008 | tf_op jit(solution)/shard_map/ppermute | solution.py:24
  90.1 12.4 %collective-permute-start.12 = (bf16[2,50,800]{2,0,1:T(2,128)(2,1)S(1)}, bf16[2,50,800]{2,0,1:T(2,128)(2,1)S(1)}, u32[]{:S(2)}, u32[]{:S(2)}) collective-permute-start(bf16[2,50,800]{2,0,1:T(2,128)(2,1)S(1)} %get-tuple-element.9), channel_id=1, source_target_pairs={{0,13},{1,12},{2,15},{3,14},{4,9},{5,8},{6,11},{7,10},{8,5},{9,4},... | collective-permute-start | bytes 480008 | tf_op jit(solution)/shard_map/ppermute | solution.py:24
  95.9 8.3 %collective-permute-start.13 = (bf16[2,50,800]{2,0,1:T(2,128)(2,1)S(1)}, bf16[2,50,800]{2,0,1:T(2,128)(2,1)S(1)}, u32[]{:S(2)}, u32[]{:S(2)}) collective-permute-start(bf16[2,50,800]{2,0,1:T(2,128)(2,1)S(1)} %get-tuple-element.8), channel_id=1, source_target_pairs={{0,14},{1,15},{2,12},{3,13},{4,10},{5,11},{6,8},{7,9},{8,6},{9,7},... | collective-permute-start | bytes 480008 | tf_op jit(solution)/shard_map/ppermute | solution.py:24
  99.1 8.5 %collective-permute-start.14 = (bf16[2,50,800]{2,0,1:T(2,128)(2,1)S(1)}, bf16[2,50,800]{2,0,1:T(2,128)(2,1)S(1)}, u32[]{:S(2)}, u32[]{:S(2)}) collective-permute-start(bf16[2,50,800]{2,0,1:T(2,128)(2,1)S(1)} %get-tuple-element.7), channel_id=1, source_target_pairs={{0,15},{1,14},{2,13},{3,12},{4,11},{5,10},{6,9},{7,8},{8,7},{9,6},... | collective-permute-start | bytes 480008 | tf_op jit(solution)/shard_map/ppermute | solution.py:24
  135.7 276.2 %copy-start.2 = (bf16[2,800,800]{2,0,1:T(2,128)(2,1)S(1)}, bf16[2,800,800]{2,0,1:T(2,128)(2,1)}, u32[]{:S(2)}) copy-start(bf16[2,800,800]{2,0,1:T(2,128)(2,1)} %copy-done.1) | copy-start | bytes 7680004
  (9 other events, 36.1 us)
Sparse Core Ops, SparseCore 0:
  35.5 87.8 all-gather.2
Sparse Core Ops, SparseCore 1:
  135.1 276.7 all-reduce.1
